TPU v7x, 128 devices: a whole 4x4x4 slice. The times are simulated.
128 devices in a mesh: dp: 2 (over core), expert: 64 (over y, z, x).
Axes of the slice: x: 4, y: 4, z: 4, core: 2. Of those that a mesh axis runs over, the one named last changes fastest.
Arguments:
- tokens: bfloat16 [16384, 4096], P(('dp', 'expert')), parts along dimension 0, may hold values from -6 to 6
- w_gate_up: bfloat16 [64, 2, 4096, 768], P('expert'), may hold values from -0.09375 to 0.09375
- w_down: bfloat16 [64, 768, 4096], P('expert'), may hold values from -0.21875 to 0.21875
- routes: int32 [16384, 8], P(('dp', 'expert')), parts along dimension 0, may hold values from 0 to 63, as said below
- gate_scaled: int32 [16384, 8], P(('dp', 'expert')), parts along dimension 0, may hold values from 1 to 1023
Outputs:
- mixed: bfloat16 [16384, 4096], P(('dp', 'expert')), parts along dimension 0
There are 2 independent parts, one for each index of `dp`. A program takes and returns all parts, laid end to end along the dimension named above; an argument that names none is the same for every part. Nothing has to cross between parts.
Inputs may be any that keep to these rules, and one draw needn't show every extreme that they name: `routes`: every row names 8 different experts. In each aligned block of 128 rows (the rows of one device) one expert, the same in every block, is named by exactly 40 rows; no other expert is named by more than 20 rows of a block, and a second expert, the same in every block, by exactly 20 rows of every block.
All inputs are finite; a program needn't handle non-finite values.
Results may differ from a plain program's by a relative error of at most 0.0057.
Values may be sent and summed in bfloat16 or wider, within the bound.
No kernel may reach another device: no remote copies, remote signals or barrier semaphores. Data moves between devices by JAX's collectives and lax.ppermute only.
A program may use at most 192 MiB of HBM per device.

v0:
```python
import jax
import jax.numpy as jnp
from jax import lax
from jax.sharding import PartitionSpec as P


def from_root(block, axis, owner):
    block = jnp.where(lax.axis_index(axis) == owner, block, jnp.zeros_like(block))
    return lax.psum(block, axis)


def expert_rows(picked, gate_up, down_proj):
    gate_val = jnp.dot(picked, gate_up[0], preferred_element_type=jnp.float32)
    up_val = jnp.dot(picked, gate_up[1], preferred_element_type=jnp.float32)
    hidden = (jax.nn.silu(gate_val) * up_val).astype(jnp.bfloat16)
    return jnp.dot(hidden, down_proj, preferred_element_type=jnp.float32).astype(jnp.bfloat16)


def body(tokens, w_gate_up, w_down, routes, gate_scaled):
    experts = lax.axis_size("expert")
    tok_rows, model_width = tokens.shape
    top_count = routes.shape[1]
    cold_cap = 5 * tok_rows * top_count // (4 * experts)
    flat_routes = routes.reshape(-1)
    onehot = (flat_routes[:, None] == jnp.arange(experts, dtype=jnp.int32)[None, :]).astype(
        jnp.int32
    )
    before = jnp.cumsum(onehot, axis=0) - onehot
    ranked = jnp.sum(before * onehot, axis=1)
    gate_up = w_gate_up[0]
    down_proj = w_down[0]
    scaled = gate_scaled.astype(jnp.float32)
    weight = scaled / jnp.sum(scaled, axis=1, keepdims=True)
    counts = jnp.sum(onehot, axis=0)
    busiest = jnp.argmax(counts)
    hot_gate_up = from_root(gate_up, "expert", busiest)
    hot_down = from_root(down_proj, "expert", busiest)
    is_hot = flat_routes == busiest
    buffer_rows = experts * cold_cap
    slot_of = jnp.where(is_hot, buffer_rows, flat_routes * cold_cap + ranked)
    token_of = jnp.arange(flat_routes.shape[0], dtype=jnp.int32) // top_count
    source_rows = jnp.zeros((buffer_rows,), jnp.int32).at[slot_of].set(token_of, mode="drop")
    outgoing = jnp.take(tokens, source_rows, axis=0).reshape(experts, cold_cap, model_width)
    incoming = lax.all_to_all(outgoing, "expert", split_axis=0, concat_axis=0, tiled=True)
    slot_count = incoming.shape[1]
    expert_out = expert_rows(incoming.reshape(-1, model_width), gate_up, down_proj)
    expert_out = expert_out.reshape(experts, slot_count, model_width)
    returned_rows = lax.all_to_all(expert_out, "expert", split_axis=0, concat_axis=0, tiled=True)
    returned_rows = returned_rows.reshape(buffer_rows, model_width)
    gathered = jnp.take(returned_rows, jnp.minimum(slot_of, buffer_rows - 1), axis=0)
    gathered = gathered.reshape(tok_rows, top_count, model_width)
    local_out = expert_rows(tokens, hot_gate_up, hot_down)
    gathered = jnp.where(is_hot.reshape(tok_rows, top_count, 1), local_out[:, None, :], gathered)
    mixed = jnp.zeros((tok_rows, model_width), jnp.float32)
    for column in range(top_count):
        mixed = mixed + weight[:, column : column + 1] * gathered[:, column].astype(jnp.float32)
    return mixed.astype(jnp.bfloat16)


def solution(mesh):
    return jax.shard_map(
        body,
        mesh=mesh,
        in_specs=(
            P(("dp", "expert"), None),
            P("expert", None, None, None),
            P("expert", None, None),
            P(("dp", "expert"), None),
            P(("dp", "expert"), None),
        ),
        out_specs=P(("dp", "expert"), None),
        check_vma=False,
    )
```

profile of v0, /device:TPU:0, one launch (start us, length us, event | category | flops | bytes accessed | tf_op | source)
XLA Modules:
  0.0 692.7 jit_solution(11836376004890335390)
XLA Ops:
  6.5 0.9 copy.16
  8.3 18.0 %reduce-window.6 = s32[64,8,128]{2,1,0:T(8,128)S(1)} reduce-window(s32[64,8,128]{2,1,0:T(8,128)S(1)} %fusion.35, s32[]{:T(128)} %constant.49.clone.1), window={size=1x1x128 pad=0_0x0_0x127_0}, to_apply=%region_5.6 | reduce-window | flops 8323072 | bytes 524292 | tf_op jit(solution)/shard_map/reduce-window
  27.9 1.9 compare_and_fusion.1
  30.6 4.3 scatter_custom_fusion
  35.0 8.4 %gather_fusion = bf16[1280,4096]{1,0:T(8,128)(2,1)} fusion(bf16[128,4096]{1,0:T(8,128)(2,1)S(1)} %copy-done, s32[2048]{0:T(1024)S(1)} %pad_clamp_fusion), kind=kCustom, calls=%fused_computation | custom fusion | bytes 20976640 | tf_op jit(solution)/shard_map/jit(_take)/gather | solution.py:43
  43.4 13.9 %gather.13 = bf16[64,20,4096]{2,1,0:T(8,128)(2,1)} reshape(bf16[1280,4096]{1,0:T(8,128)(2,1)} %gather_fusion) | data formatting | bytes 20971520 | tf_op jit(solution)/shard_map/jit(_take)/gather | solution.py:43
  57.4 10.7 %broadcast_select_fusion = bf16[64,20,4096]{2,1,0:T(8,128)(2,1)} fusion(bf16[64,20,4096]{2,1,0:T(8,128)(2,1)} %gather.13, pred[64,20]{1,0:T(8,128)(4,1)S(1)} %broadcast_in_dim.67), kind=kLoop, calls=%fused_computation.5 | loop fusion | flops 5242880 | bytes 20972800 | tf_op jit(solution)/shard_map/jit(_take)/select_n | solution.py:43
  68.1 11.7 %all-to-all-start = ((bf16[64,20,4096]{2,1,0:T(8,128)(2,1)}), bf16[64,20,4096]{2,1,0:T(8,128)(2,1)}, u32[]{:S(2)}, u32[]{:S(2)}) async-start(bf16[64,20,4096]{2,1,0:T(8,128)(2,1)} %broadcast_select_fusion), calls=%async_computation | async-start | bytes 25165824 | tf_op jit(solution)/shard_map/all_to_all | solution.py:44
  80.6 5.8 bitcast_select_fusion
  86.4 5.5 select_bitcast_fusion
  92.0 173.1 %all-to-all-done = bf16[64,20,4096]{2,1,0:T(8,128)(2,1)} async-done(((bf16[64,20,4096]{2,1,0:T(8,128)(2,1)}), bf16[64,20,4096]{2,1,0:T(8,128)(2,1)}, u32[]{:S(2)}, u32[]{:S(2)}) %all-to-all-start) | async-done | bytes 10485792 | tf_op jit(solution)/shard_map/all_to_all | solution.py:44
  265.1 14.3 %reshape.148 = bf16[1280,4096]{1,0:T(8,128)(2,1)} reshape(bf16[64,20,4096]{2,1,0:T(8,128)(2,1)} %all-to-all-done) | data formatting | bytes 20971520 | tf_op jit(solution)/shard_map/reshape | solution.py:46
  279.4 14.8 %fusion.5 = f32[1280,768]{1,0:T(8,128)} fusion(bf16[1280,4096]{1,0:T(8,128)(2,1)} %reshape.148, bf16[1,2,4096,768]{3,2,1,0:T(8,128)(2,1)} %param.6), kind=kOutput, calls=%fused_computation.14 | convolution fusion | flops 8053063680 | bytes 20709376 | tf_op jit(solution)/shard_map/dot_general | solution.py:13
  294.1 11.6 %fusion.13 = bf16[1280,768]{1,0:T(8,128)(2,1)S(1)} fusion(bf16[1280,4096]{1,0:T(8,128)(2,1)S(1)} %copy-done.1, bf16[1,2,4096,768]{3,2,1,0:T(8,128)(2,1)} %param.6, f32[1280,768]{1,0:T(8,128)} %fusion.5), kind=kOutput, calls=%fused_computation.22 | convolution fusion | flops 8058961920 | bytes 22675456 | tf_op jit(solution)/shard_map/dot_general | solution.py:14
  305.8 10.6 %convolution_convert_fusion = bf16[1280,4096]{1,0:T(8,128)(2,1)} fusion(bf16[1280,768]{1,0:T(8,128)(2,1)S(1)} %fusion.13, bf16[1,768,4096]{2,1,0:T(8,128)(2,1)S(1)} %bitcast.120), kind=kOutput, calls=%fused_computation.3 | convolution fusion | flops 8058306560 | bytes 18743296 | tf_op jit(solution)/shard_map/dot_general | solution.py:16
  316.4 13.9 %reshape.149 = bf16[64,20,4096]{2,1,0:T(8,128)(2,1)} reshape(bf16[1280,4096]{1,0:T(8,128)(2,1)} %convolution_convert_fusion) | data formatting | bytes 20971520 | tf_op jit(solution)/shard_map/reshape | solution.py:47
  330.3 53.8 %all-to-all-start.1 = ((bf16[64,20,4096]{2,1,0:T(8,128)(2,1)}), bf16[64,20,4096]{2,1,0:T(8,128)(2,1)}, u32[]{:S(2)}, u32[]{:S(2)}) async-start(bf16[64,20,4096]{2,1,0:T(8,128)(2,1)} %reshape.149), calls=%async_computation.1 | async-start | bytes 25165824 | tf_op jit(solution)/shard_map/all_to_all | solution.py:48
  384.3 234.0 %all-reduce.3.cloned.1.call-done = (bf16[768,4096]{1,0:T(8,128)(2,1)}, bf16[2,4096,768]{2,1,0:T(8,128)(2,1)}) async-done(((bf16[768,4096]{1,0:T(8,128)(2,1)}, bf16[2,4096,768]{2,1,0:T(8,128)(2,1)}), (bf16[768,4096]{1,0:T(8,128)(2,1)}, bf16[2,4096,768]{2,1,0:T(8,128)(2,1)})) %all-reduce.3.cloned.1.call-update) | async-done | bytes 18874384 | tf_op jit(solution)/shard_map/psum | solution.py:9
  618.2 4.6 fusion.24
  622.8 8.9 %convolution_convert_fusion.1 = bf16[128,4096]{1,0:T(8,128)(2,1)S(1)} fusion(bf16[768,4096]{1,0:T(8,128)(2,1)} %get-tuple-element.9, bf16[128,4096]{1,0:T(8,128)(2,1)S(1)} %copy-done, bf16[2,4096,768]{2,1,0:T(8,128)(2,1)} %get-tuple-element.10, f32[128,768]{0,1:T(8,128)S(1)} %fusion.24), kind=kOutput, calls=%fused_computation.20 | convolution fusion | flops 1611726848 | bytes 15073280 | tf_op jit(solution)/shard_map/dot_general | solution.py:16
  631.7 14.2 %reshape.150 = bf16[1280,4096]{1,0:T(8,128)(2,1)} reshape(bf16[64,20,4096]{2,1,0:T(8,128)(2,1)} %all-to-all-done.1) | data formatting | bytes 20971520 | tf_op jit(solution)/shard_map/reshape | solution.py:49
  646.0 20.5 %gather_fusion.1 = bf16[1024,4096]{1,0:T(8,128)(2,1)} fusion(bf16[1280,4096]{1,0:T(8,128)(2,1)} %reshape.150, s32[1024]{0:T(1024)S(1)} %broadcast_clamp_fusion), kind=kCustom, calls=%fused_computation.1 | custom fusion | bytes 16781312 | tf_op jit(solution)/shard_map/jit(_take)/gather | solution.py:50
  666.4 16.3 %fusion = bf16[128,8,4096]{2,0,1:T(8,128)(2,1)S(1)} fusion(bf16[128,8,4096]{2,1,0:T(8,128)(2,1)} %bitcast.118, pred[128,8]{0,1:T(8,128)(4,1)S(1)} %copy-done.5, pred[128,8]{0,1:T(8,128)(4,1)S(1)} %copy-done.4, bf16[128,4096]{1,0:T(8,128)(2,1)S(1)} %convolution_convert_fusion.1), kind=kLoop, calls=%fused_computation.7 | loop fusion | flops 8388608 | bytes 17827840 | tf_op jit(solution)/shard_map/jit(_where)/select_n | solution.py:53
  682.8 3.1 fusion.17
  (48 shorter events, 3.7 us)
Async XLA Ops:
  6.5 28.4 %copy-start = (bf16[128,4096]{1,0:T(8,128)(2,1)S(1)}, bf16[128,4096]{1,0:T(8,128)(2,1)}, u32[]{:S(2)}) copy-start(bf16[128,4096]{1,0:T(8,128)(2,1)} %param.5) | copy-start | bytes 3145732
  29.7 0.5 copy-start.3
  68.1 197.0 %all-to-all-start = ((bf16[64,20,4096]{2,1,0:T(8,128)(2,1)}), bf16[64,20,4096]{2,1,0:T(8,128)(2,1)}, u32[]{:S(2)}, u32[]{:S(2)}) async-start(bf16[64,20,4096]{2,1,0:T(8,128)(2,1)} %broadcast_select_fusion), calls=%async_computation | async-start | bytes 25165824 | tf_op jit(solution)/shard_map/all_to_all | solution.py:44
  79.8 538.4 %all-reduce.3.cloned.1.call-start = ((), (), s32[]{:S(2)}) async-start(), calls=%async_computation.2 | async-start | bytes 37748736 | tf_op jit(solution)/shard_map/psum | solution.py:9
  279.4 14.8 %copy-start.1 = (bf16[1280,4096]{1,0:T(8,128)(2,1)S(1)}, bf16[1280,4096]{1,0:T(8,128)(2,1)}, u32[]{:S(2)}) copy-start(bf16[1280,4096]{1,0:T(8,128)(2,1)} %reshape.148) | copy-start | bytes 31457284
  279.4 26.4 %slice-start = ((s8[6291456]{0:T(1024)(128)(4,1)}), s8[4194304]{0:T(1024)(128)(4,1)S(1)}, s32[]{:S(2)}) async-start(s8[6291456]{0:T(1024)(128)(4,1)} %bitcast.119), calls=%async_computation.3 | async-start | bytes 8388608
  294.1 11.6 %slice-start.1 = ((s8[6291456]{0:T(1024)(128)(4,1)}), s8[2097152]{0:T(1024)(128)(4,1)S(1)}, s32[]{:S(2)}) async-start(s8[6291456]{0:T(1024)(128)(4,1)} %bitcast.119), calls=%async_computation.4 | async-start | bytes 4194304
  330.3 53.9 %copy-start.2 = (s32[128,8]{0,1:T(8,128)S(1)}, s32[128,8]{0,1:T(8,128)}, u32[]{:S(2)}) copy-start(s32[128,8]{0,1:T(8,128)} %param.9) | copy-start | bytes 12292
  330.3 301.4 %all-to-all-start.1 = ((bf16[64,20,4096]{2,1,0:T(8,128)(2,1)}), bf16[64,20,4096]{2,1,0:T(8,128)(2,1)}, u32[]{:S(2)}, u32[]{:S(2)}) async-start(bf16[64,20,4096]{2,1,0:T(8,128)(2,1)} %reshape.149), calls=%async_computation.1 | async-start | bytes 25165824 | tf_op jit(solution)/shard_map/all_to_all | solution.py:48
  645.9 20.5 %copy-start.4 = (pred[128,8]{0,1:T(8,128)(4,1)S(1)}, pred[128,8]{0,1:T(8,128)(4,1)}, u32[]{:S(2)}) copy-start(pred[128,8]{0,1:T(8,128)(4,1)} %copy-done.3) | copy-start | bytes 3076
  645.9 20.5 %copy-start.5 = (pred[128,8]{0,1:T(8,128)(4,1)S(1)}, pred[128,8]{0,1:T(8,128)(4,1)}, u32[]{:S(2)}) copy-start(pred[128,8]{0,1:T(8,128)(4,1)} %get-tuple-element.11) | copy-start | bytes 3076
Sparse Core Ops, SparseCore 0:
  92.1 526.0 all-reduce.2
where the time goes:
time: 702 us; the launch traced here: 693 us
  waiting for transfers between devices  407 us (58%)
  local copies, waits for them, and re-layouts  92 us (13%)
  starting transfers between devices  65.8 us (9%)
  other arithmetic  63.2 us (9%)
  matrix products  50.5 us (7%)
  between operations  14.2 us (2%)
    psum x1, waiting for transfers between devices, from_root(): return lax.psum(block, axis)  234 us
    all_to_all x1, waiting for transfers between devices, body(): lax.all_to_all(outgoing, 'expert', split_axis=0, concat_axis=0, tiled=True)  173 us
    all_to_all x1, starting transfers between devices, body(): lax.all_to_all(expert_out, 'expert', split_axis=0, concat_axis=0, tiled=T...  53.8 us
    gather x2, local copies, waits for them, and re-layouts, body(): jnp.take(tokens, source_rows, axis=0)  22.3 us
    gather x1, local copies, waits for them, and re-layouts, body(): jnp.take(returned_rows, jnp.minimum(slot_of, buffer_rows - 1), axis=0)  20.5 us
    dot_general x2, matrix products, expert_rows(): jnp.dot(hidden, down_proj, preferred_element_type=jnp.float32)  19.5 us
    dot_general x2, matrix products, expert_rows(): gate_val = jnp.dot(picked, gate_up[0], preferred_element_type=jnp.float32)  19.4 us
    another operation x3, other arithmetic  18.2 us
  transfers between devices with their start and end apart: 3, of which 2 were waited for; matrix products, arithmetic and copies ran while one was open for 13% of the time, Pallas kernels for 0%

commit v1 on v0

v1 whole, which is shorter than its diff:
```python
import jax
import jax.numpy as jnp
from jax import lax
from jax.sharding import PartitionSpec as P

def expert_sums(picked, gate, up, down):
    gate_val = jnp.dot(picked, gate, preferred_element_type=jnp.float32)
    up_val = jnp.dot(picked, up, preferred_element_type=jnp.float32)
    hidden = (jax.nn.silu(gate_val) * up_val).astype(jnp.bfloat16)
    return jnp.dot(hidden, down, preferred_element_type=jnp.float32)


def body(tokens, w_gate_up, w_down, routes, gate_scaled):
    experts = lax.axis_size("expert")
    tok_rows, width = tokens.shape
    slots = 24
    gate, up, down = w_gate_up[0, 0], w_gate_up[0, 1], w_down[0]

    routes_t = routes.T
    expert_ids = jnp.arange(experts, dtype=jnp.int32)
    hit = routes_t[:, None, :] == expert_ids[None, :, None]
    named = jnp.any(hit, axis=0)
    earlier = jnp.arange(tok_rows)[:, None] < jnp.arange(tok_rows)[None, :]
    rank = jnp.dot(
        named.astype(jnp.bfloat16), earlier.astype(jnp.bfloat16), preferred_element_type=jnp.float32
    ).astype(jnp.int32)
    counts = jnp.sum(named.astype(jnp.int32), axis=1)
    busiest = jnp.argmax(counts).astype(jnp.int32)
    scaled = gate_scaled.T.astype(jnp.float32)
    weight = scaled / jnp.sum(scaled, axis=0, keepdims=True)
    weight_of = jnp.sum(jnp.where(hit, weight[:, None, :], 0.0), axis=0)
    hot_weight = jnp.sum(jnp.where(routes_t == busiest, weight, 0.0), axis=0)
    cold = named & (expert_ids != busiest)[:, None]
    slot_of = jnp.where(cold, rank, -1)

    owner = lax.axis_index("expert") == busiest
    own = [w_gate_up[0], down]
    hot_gate_up, hot_down = lax.psum([jnp.where(owner, w, jnp.zeros_like(w)) for w in own], "expert")

    at_slot = slot_of[:, None, :] == jnp.arange(slots, dtype=jnp.int32)[None, :, None]
    pick = at_slot.astype(jnp.bfloat16).reshape(experts * slots, tok_rows)
    outgoing = jnp.dot(pick, tokens, preferred_element_type=jnp.float32).astype(jnp.bfloat16)
    incoming = lax.all_to_all(
        outgoing.reshape(experts, slots, width), "expert", split_axis=0, concat_axis=0, tiled=True
    )
    expert_out = expert_sums(incoming.reshape(experts * slots, width), gate, up, down).astype(
        jnp.bfloat16
    )
    returned = lax.all_to_all(
        expert_out.reshape(experts, slots, width), "expert", split_axis=0, concat_axis=0, tiled=True
    ).reshape(experts * slots, width)

    mix = jnp.where(at_slot, weight_of[:, None, :], 0.0).reshape(experts * slots, tok_rows)
    mix_top = lax.reduce_precision(mix, 8, 7)
    mix_hi = mix_top.astype(jnp.bfloat16)
    mix_lo = (mix - mix_top).astype(jnp.bfloat16)
    both = lax.dot_general(
        jnp.concatenate([mix_hi, mix_lo], axis=1),
        returned,
        (((0,), (0,)), ((), ())),
        preferred_element_type=jnp.float32,
    )
    hot_out = expert_sums(tokens, hot_gate_up[0], hot_gate_up[1], hot_down).astype(jnp.bfloat16)
    mixed = both[:tok_rows] + both[tok_rows:] + hot_weight[:, None] * hot_out.astype(jnp.float32)
    return mixed.astype(jnp.bfloat16)


def solution(mesh):
    return jax.shard_map(
        body,
        mesh=mesh,
        in_specs=(
            P(("dp", "expert"), None),
            P("expert", None, None, None),
            P("expert", None, None),
            P(("dp", "expert"), None),
            P(("dp", "expert"), None),
        ),
        out_specs=P(("dp", "expert"), None),
        check_vma=False,
    )
```

time: 702 us -> 601 us (0.86)
  local copies, waits for them, and re-layouts: 92 us -> 0.11 us
  other arithmetic: 63.2 us -> 14.8 us
  waiting for transfers between devices: 407 us -> 434 us
  matrix products: 50.5 us -> 74.1 us
    gather x3 -> x0, local copies, waits for them, and re-layouts: 42.7 us -> none  [the longest x2 22.3 us: body(): jnp.take(tokens, source_rows, axis=0)]
    reshape x3 -> x0, local copies, waits for them, and re-layouts: 42.4 us -> none  [the longest x1 14.3 us: body(): incoming.reshape(-1, model_width)]
    psum x1, waiting for transfers between devices: 234 us -> 262 us  [body(): lax.psum([jnp.where(owner, w, jnp.zeros_like(w)) for w in own], 'expert')]
    select_n x7 -> x2, other arithmetic: 38.4 us -> 11.3 us  [body(): jnp.where(owner, w, jnp.zeros_like(w))]
    dot_general x5 -> x8, matrix products: 50.5 us -> 74.1 us  [the longest x2 23.3 us: expert_sums(): return jnp.dot(hidden, down, preferred_element_type=jnp.float32)]
    another operation x4 -> x1, other arithmetic: 18.9 us -> 0.68 us  [body(): busiest = jnp.argmax(counts).astype(jnp.int32)]
  transfers between devices with their start and end apart: 3 -> 3, of which waited for: 2 -> 2; matrix products, arithmetic and copies ran while one was open for 13% -> 10% of each run, Pallas kernels for 0% -> 0%
where the time goes in v1:
time: 601 us; the launch traced here: 599 us
  waiting for transfers between devices  434 us (72%)
  matrix products  74.1 us (12%)
  starting transfers between devices  61.4 us (10%)
  other arithmetic  14.8 us (2%)
  between operations  14.2 us (2%)
    psum x1, waiting for transfers between devices, body(): lax.psum([jnp.where(owner, w, jnp.zeros_like(w)) for w in own], 'expert')  262 us
    all_to_all x1, waiting for transfers between devices, body(): lax.all_to_all(outgoing.reshape(experts, slots, width), 'expert', split_a...  172 us
    all_to_all x1, starting transfers between devices, body(): lax.all_to_all(expert_out.reshape(experts, slots, width), 'expert', split...  49.5 us
    dot_general x2, matrix products, expert_sums(): return jnp.dot(hidden, down, preferred_element_type=jnp.float32)  23.3 us
    dot_general x2, matrix products, expert_sums(): gate_val = jnp.dot(picked, gate, preferred_element_type=jnp.float32)  20.3 us
    dot_general x1, matrix products, expert_sums(): up_val = jnp.dot(picked, up, preferred_element_type=jnp.float32)  14.4 us
  transfers between devices with their start and end apart: 3, of which 2 were waited for; matrix products, arithmetic and copies ran while one was open for 10% of the time, Pallas kernels for 0%

profile of v1, /device:TPU:0, one launch (start us, length us, event | category | flops | bytes accessed | tf_op | source)
XLA Modules:
  0.0 598.6 jit_solution(16081414150689924342)
XLA Ops:
  6.5 0.8 fusion.30
  7.4 0.1 convert_reduce_fusion
  7.5 0.7 iota_reduce_fusion
  8.1 0.6 iota_compare_fusion.3
  8.8 0.1 fusion.19
  8.9 0.1 eq.51
  9.0 0.3 bitcast_compare_fusion
  9.3 6.2 %convolution_convert_fusion.1 = bf16[1536,4096]{1,0:T(8,128)(2,1)} fusion(pred[1536,128]{1,0:T(32,128)(4,1)S(1)} %bitcast_compare_fusion, bf16[128,4096]{1,0:T(8,128)(2,1)S(1)} %copy-done), kind=kOutput, calls=%fused_computation.1 | convolution fusion | flops 1616904192 | bytes 13828096 | tf_op jit(solution)/shard_map/dot_general | solution.py:42
  15.6 11.7 %all-to-all-start = ((bf16[64,24,4096]{2,1,0:T(8,128)(2,1)}), bf16[64,24,4096]{2,1,0:T(8,128)(2,1)}, u32[]{:S(2)}, u32[]{:S(2)}) async-start(bf16[64,24,4096]{2,1,0:T(8,128)(2,1)} %bitcast.71), calls=%async_computation | async-start | bytes 25165824 | tf_op jit(solution)/shard_map/all_to_all | solution.py:43
  27.3 0.2 all-reduce.3.cloned.1.call-start
  28.2 5.8 bitcast_select_fusion
  34.0 5.5 select_bitcast_fusion
  39.5 0.0 all-reduce.3.cloned.1.call-update
  39.5 171.8 %all-to-all-done = bf16[64,24,4096]{2,1,0:T(8,128)(2,1)} async-done(((bf16[64,24,4096]{2,1,0:T(8,128)(2,1)}), bf16[64,24,4096]{2,1,0:T(8,128)(2,1)}, u32[]{:S(2)}, u32[]{:S(2)}) %all-to-all-start) | async-done | bytes 12582944 | tf_op jit(solution)/shard_map/all_to_all | solution.py:43
  211.3 14.4 %fusion.3 = f32[1536,768]{1,0:T(8,128)S(1)} fusion(bf16[1536,4096]{1,0:T(8,128)(2,1)} %bitcast.5, bf16[1,2,4096,768]{3,2,1,0:T(8,128)(2,1)} %param.6), kind=kOutput, calls=%fused_computation.9 | convolution fusion | flops 9663676416 | bytes 23592960 | tf_op jit(solution)/shard_map/dot_general | solution.py:8
  225.7 15.7 %multiply_convert_fusion = bf16[1536,768]{1,0:T(8,128)(2,1)S(1)} fusion(f32[1536,768]{1,0:T(8,128)S(1)} %fusion.3, bf16[1536,4096]{1,0:T(8,128)(2,1)} %bitcast.5, bf16[1,2,4096,768]{3,2,1,0:T(8,128)(2,1)} %param.6), kind=kOutput, calls=%fused_computation.20 | convolution fusion | flops 9670754304 | bytes 25952256 | tf_op jit(solution)/shard_map/dot_general | solution.py:7
  241.5 12.3 %convolution_convert_fusion = bf16[1536,4096]{1,0:T(8,128)(2,1)} fusion(bf16[1536,768]{1,0:T(8,128)(2,1)S(1)} %multiply_convert_fusion, bf16[1,768,4096]{2,1,0:T(8,128)(2,1)S(1)} %bitcast.74), kind=kOutput, calls=%fused_computation | convolution fusion | flops 9669967872 | bytes 21233664 | tf_op jit(solution)/shard_map/dot_general | solution.py:10
  253.8 49.5 %all-to-all-start.1 = ((bf16[64,24,4096]{2,1,0:T(8,128)(2,1)}), bf16[64,24,4096]{2,1,0:T(8,128)(2,1)}, u32[]{:S(2)}, u32[]{:S(2)}) async-start(bf16[64,24,4096]{2,1,0:T(8,128)(2,1)} %bitcast.72), calls=%async_computation.1 | async-start | bytes 25165824 | tf_op jit(solution)/shard_map/all_to_all | solution.py:49
  303.3 0.7 select_reduce_fusion.1
  304.0 0.3 reduce-precision_convert_fusion
  304.3 262.1 %all-reduce.3.cloned.1.call-done = (bf16[768,4096]{1,0:T(8,128)(2,1)}, bf16[2,4096,768]{2,1,0:T(8,128)(2,1)}) async-done(((bf16[768,4096]{1,0:T(8,128)(2,1)}, bf16[2,4096,768]{2,1,0:T(8,128)(2,1)}), (bf16[768,4096]{1,0:T(8,128)(2,1)}, bf16[2,4096,768]{2,1,0:T(8,128)(2,1)})) %all-reduce.3.cloned.1.call-update) | async-done | bytes 18874384 | tf_op jit(solution)/shard_map/psum | solution.py:38
  566.4 4.6 fusion.15
  571.0 9.6 %fusion.21 = f32[256,4096]{1,0:T(8,128)} fusion(bf16[1536,4096]{1,0:T(8,128)(2,1)} %bitcast.10, bf16[1536,128]{1,0:T(8,128)(2,1)S(1)} %get-tuple-element.12, bf16[1536,128]{1,0:T(8,128)(2,1)S(1)} %get-tuple-element.11), kind=kOutput, calls=%fused_computation.31 | convolution fusion | flops 3222798336 | bytes 17563648 | tf_op jit(solution)/shard_map/dot_general | solution.py:57
  580.7 11.1 %fusion.12 = bf16[128,4096]{1,0:T(8,128)(2,1)} fusion(bf16[768,4096]{1,0:T(8,128)(2,1)} %get-tuple-element.7, f32[256,4096]{1,0:T(8,128)} %fusion.21, f32[128]{0:T(128)S(1)} %get-tuple-element.9, bf16[128,4096]{1,0:T(8,128)(2,1)S(1)} %copy-done, bf16[2,4096,768]{2,1,0:T(8,128)(2,1)} %get-tuple-element.8, f32[128,768]{0,1:T(8,128)S(1)} %fusion.15), kind=kOutput, calls=%fused_computation.19 | convolution fusion | flops 1614348288 | bytes 19268096 | tf_op jit(solution)/shard_map/dot_general | solution.py:10
  (15 shorter events, 0.1 us)
Async XLA Ops:
  6.5 2.8 copy-start
  15.6 195.7 %all-to-all-start = ((bf16[64,24,4096]{2,1,0:T(8,128)(2,1)}), bf16[64,24,4096]{2,1,0:T(8,128)(2,1)}, u32[]{:S(2)}, u32[]{:S(2)}) async-start(bf16[64,24,4096]{2,1,0:T(8,128)(2,1)} %bitcast.71), calls=%async_computation | async-start | bytes 25165824 | tf_op jit(solution)/shard_map/all_to_all | solution.py:43
  27.3 539.1 %all-reduce.3.cloned.1.call-start = ((), (), s32[]{:S(2)}) async-start(), calls=%async_computation.2 | async-start | bytes 37748736 | tf_op jit(solution)/shard_map/psum | solution.py:38
  211.3 30.2 %slice-start = ((s8[6291456]{0:T(1024)(128)(4,1)}), s8[4194304]{0:T(1024)(128)(4,1)S(1)}, s32[]{:S(2)}) async-start(s8[6291456]{0:T(1024)(128)(4,1)} %bitcast.73), calls=%async_computation.3 | async-start | bytes 8388608
  225.7 15.8 %slice-start.1 = ((s8[6291456]{0:T(1024)(128)(4,1)}), s8[2097152]{0:T(1024)(128)(4,1)S(1)}, s32[]{:S(2)}) async-start(s8[6291456]{0:T(1024)(128)(4,1)} %bitcast.73), calls=%async_computation.4 | async-start | bytes 4194304
  253.8 49.5 %copy-start.2 = (s32[128,8]{0,1:T(8,128)S(1)}, s32[128,8]{0,1:T(8,128)}, u32[]{:S(2)}) copy-start(s32[128,8]{0,1:T(8,128)} %param.9) | copy-start | bytes 12292
  253.8 49.5 %copy-start.1 = (s32[128,8]{0,1:T(8,128)S(1)}, s32[128,8]{0,1:T(8,128)}, u32[]{:S(2)}) copy-start(s32[128,8]{0,1:T(8,128)} %param.8) | copy-start | bytes 12292
  253.8 317.3 %all-to-all-start.1 = ((bf16[64,24,4096]{2,1,0:T(8,128)(2,1)}), bf16[64,24,4096]{2,1,0:T(8,128)(2,1)}, u32[]{:S(2)}, u32[]{:S(2)}) async-start(bf16[64,24,4096]{2,1,0:T(8,128)(2,1)} %bitcast.72), calls=%async_computation.1 | async-start | bytes 25165824 | tf_op jit(solution)/shard_map/all_to_all | solution.py:49
Sparse Core Ops, SparseCore 0:
  39.6 526.7 all-reduce.2
